TPU v7x, 32 devices: a whole 2x2x4 slice. The times are simulated.
32 devices in a mesh: groups: 2 (over x), img: 16 (over z, y, core).
Axes of the slice: x: 2, y: 2, z: 4, core: 2. Of those that a mesh axis runs over, the one named last changes fastest.
Arguments:
- images: bfloat16 [256, 4608], P(('groups', 'img')), parts along dimension 0, may hold values from -64 to 64
- class_refs: bfloat16 [96, 4608], P('groups', 'img'), parts along dimension 0, may hold values from -0.6 to 0.6
- sigma2: float32 [32, 16], P('groups'), parts along dimension 0, may hold values from 0.5 to 18
- ctf_group: int32 [256], P(('groups', 'img')), parts along dimension 0, may hold values from 0 to 15, as said below
- defocus_bin: int32 [256], P(('groups', 'img')), parts along dimension 0, may hold values from 0 to 31
Outputs:
- new_refs: float32 [96, 4608], P('groups', 'img'), parts along dimension 0
There are 2 independent parts, one for each index of `groups`. A program takes and returns all parts, laid end to end along the dimension named above; each array names one. Nothing has to cross between parts.
Inputs may be any that keep to these rules, and one draw needn't show every extreme that they name: `ctf_group`: never falls from one image to the next; every group appears.
All inputs are finite; a program needn't handle non-finite values.
Results may differ from a plain program's by a relative error of at most 0.0084.
Values may be sent and summed in bfloat16 or wider, within the bound.
A program may use at most 128 MiB of HBM per device.

v0:
```python
import math

import jax
import jax.numpy as jnp
import numpy as np
from jax import lax
from jax.experimental import pallas as pl
from jax.experimental.pallas import tpu as pltpu
from jax.sharding import PartitionSpec as P

CLASSES = 48
ROT = 36
SHELLS = 16
ANG = 144
REACH = 3
SHIFTS = 49
BINS = 32
NGROUP = 16


LANES = 128
PARTS = 2 * SHELLS
SPAN = ANG // ROT * PARTS
WIDTH = ROT * SPAN
SIDE = 2 * REACH + 1
SLOTS = SIDE + 1
BIG = 1e30


def phase_parts():
    offsets = np.arange(SIDE) - REACH
    angles = 2.0 * np.pi * np.arange(ANG) / ANG
    radius = (np.arange(SHELLS) + 1.0) / (2.0 * SHELLS)
    tables = []
    for direction in (np.cos(angles), np.sin(angles)):
        phase = 2.0 * np.pi * offsets[:, None, None] * direction[None, :, None] * radius
        cosine, sine = np.cos(phase), np.sin(phase)
        tables.append(np.stack([cosine, cosine], axis=2).reshape(SIDE, WIDTH))
        tables.append(np.stack([-sine, sine], axis=2).reshape(SIDE, WIDTH))
    return np.stack(tables).astype(np.float32)


def ctf_lanes():
    radius = (np.arange(SHELLS) + 1.0) / (2.0 * SHELLS)
    defocus = 1.0 + np.arange(BINS) / BINS
    table = -np.sin(80.0 * defocus[:, None] * radius**2 + 0.1)
    return np.tile(table, (1, SPAN // SHELLS)).astype(np.float32)


def fold_lanes(row, count_img, combine):
    cols = row.shape[1]
    total = row[:, :LANES]
    for start in range(LANES, cols, LANES):
        total = combine(total, row[:, start : start + LANES])
    reach = count_img
    while reach < LANES:
        total = combine(total, pltpu.roll(total, reach, 1))
        reach *= 2
    return jnp.concatenate([total] * (cols // LANES), axis=1)


def packing(width):
    full, tail = width // LANES, width % LANES
    groups = 3 if tail and 3 * tail <= LANES and CLASSES % 48 == 0 else 1
    return full, tail, groups


def packed_rows(width):
    full, tail, groups = packing(width)
    return full * CLASSES + (CLASSES // groups if tail else 0)


def pack(block):
    full, tail, groups = packing(block.shape[1])
    columns = [block[:, index * LANES : (index + 1) * LANES] for index in range(full)]
    if tail:
        rest = block[:, full * LANES :]
        size = CLASSES // groups
        pieces = [rest[index * size : (index + 1) * size] for index in range(groups)]
        spare = LANES - groups * tail
        if spare:
            pieces.append(jnp.zeros((size, spare), block.dtype))
        columns.append(jnp.concatenate(pieces, axis=1))
    return jnp.concatenate(columns, axis=0)


def unpack(block, width):
    full, tail, groups = packing(width)
    columns = [block[index * CLASSES : (index + 1) * CLASSES] for index in range(full)]
    if tail:
        rest = block[full * CLASSES :]
        columns.append(
            jnp.concatenate(
                [rest[:, index * tail : (index + 1) * tail] for index in range(groups)], axis=0
            )
        )
    return jnp.concatenate(columns, axis=1)


def em_kernel(
    count_dev,
    img_ref,
    refs_ref,
    sigma_ref,
    group_ref,
    bin_ref,
    ctf_ref,
    phase_ref,
    out_ref,
    feats,
    twice,
    scores,
    post,
    acc,
    turned_img,
    turned,
    turned_field,
    sw_ref,
    partial,
    mine,
    got,
    pay,
    mid,
    mixed,
    final,
    near_send,
    near_recv,
    far_send,
    far_recv,
    pair_send,
    pair_recv,
    last_send,
    last_recv,
):
    rows = CLASSES
    count_img = img_ref.shape[0]
    share = refs_ref.shape[1]
    cols = feats.shape[0]
    half = count_dev // 2
    packed = share + 8
    piece = min(share, ANG)
    pieces = share // piece
    me = lax.axis_index("img")
    core = lax.rem(me, 2)
    place = lax.div(me, 2)
    partner = me + 1 - 2 * core

    def ahead(offset):
        return lax.rem(place + offset, half)

    def behind(offset):
        return lax.rem(place + half - offset, half)

    barrier = pltpu.get_barrier_semaphore()
    for offset in range(1, half):
        pl.semaphore_signal(
            barrier,
            inc=1,
            device_id={"img": 2 * ahead(offset) + core},
            device_id_type=pl.DeviceIdType.MESH,
        )
    pl.semaphore_signal(
        barrier, inc=1, device_id={"img": partner}, device_id_type=pl.DeviceIdType.MESH
    )
    pl.semaphore_wait(barrier, half)

    def remote(source, target, send, recv, device):
        return pltpu.make_async_remote_copy(
            src_ref=source,
            dst_ref=target,
            send_sem=send,
            recv_sem=recv,
            device_id={"img": device},
            device_id_type=pl.DeviceIdType.MESH,
        )

    mine[...] = pack(refs_ref[...].astype(jnp.float32)).astype(jnp.bfloat16)

    far = [
        remote(
            mine,
            got.at[me],
            far_send.at[offset],
            far_recv.at[offset],
            2 * ahead(offset) + core,
        )
        for offset in range(1, half)
    ]
    near = [remote(mine, got.at[me], near_send.at[0], near_recv.at[0], partner)]
    for copy in far + near:
        copy.start()

    for part in range(PARTS):
        block = img_ref[:, part * ANG : (part + 1) * ANG].astype(jnp.float32)
        turned_img[pl.ds(part, ANG, stride=PARTS), :] = block.T
    repeats = SPAN // SHELLS
    noise = jnp.concatenate([sigma_ref[...]] * repeats, axis=1)

    def pick(ids, table):
        hot = ids == lax.broadcasted_iota(jnp.int32, (table.shape[0], count_img), 0)
        return lax.dot_general(
            hot.astype(jnp.float32),
            table,
            (((0,), (0,)), ((), ())),
            precision=lax.Precision.HIGHEST,
            preferred_element_type=jnp.float32,
        )

    ctf = pick(bin_ref[...], ctf_ref[...])
    noise = pick(group_ref[...], noise)
    weight = ctf / noise
    image_col = lax.rem(lax.broadcasted_iota(jnp.int32, (count_img, cols), 1), count_img)
    image_hot = image_col == lax.broadcasted_iota(jnp.int32, (count_img, cols), 0)
    sw_ref[...] = lax.dot_general(
        ctf * ctf / noise,
        image_hot.astype(jnp.float32),
        (((0,), (0,)), ((), ())),
        precision=lax.Precision.HIGHEST,
        preferred_element_type=jnp.float32,
    )
    lane = lax.broadcasted_iota(jnp.int32, (count_img, WIDTH), 1)
    real_lane = lax.rem(lane, PARTS) < SHELLS

    def swap(value):
        return jnp.where(
            real_lane, pltpu.roll(value, WIDTH - SHELLS, 1), pltpu.roll(value, SHELLS, 1)
        )

    filtered = jnp.concatenate(
        [turned_img[q * SPAN : (q + 1) * SPAN, :].T * weight for q in range(ROT)], axis=1
    )
    partial[0] = filtered
    partial[1] = swap(filtered)
    group = SLOTS * count_img

    def feature_step(step, carry):
        moved = (
            partial[0] * phase_ref[0, pl.ds(step, 1), :]
            + partial[1] * phase_ref[1, pl.ds(step, 1), :]
        )
        partial[2] = moved
        partial[3] = swap(moved)
        start = pl.multiple_of(step * group, group)
        for slot in range(0, SLOTS, 2):
            pair = []
            for shift in (slot, slot + 1):
                if shift < SIDE:
                    pair.append(
                        partial[2] * phase_ref[2, shift : shift + 1, :]
                        + partial[3] * phase_ref[3, shift : shift + 1, :]
                    )
                else:
                    pair.append(jnp.zeros((count_img, WIDTH), jnp.float32))
            feats[pl.ds(start + slot * count_img, 2 * count_img), :] = jnp.concatenate(
                pair, axis=0
            ).astype(jnp.bfloat16)
        return carry

    lax.fori_loop(0, SIDE, feature_step, 0)
    feats[SIDE * group :, :] = jnp.zeros((cols - SIDE * group, WIDTH), jnp.bfloat16)

    def place_refs(block, source):
        for index in range(pieces):
            first = source * share + index * piece
            start = lax.rem(first, ANG) * PARTS + lax.div(first, ANG)
            turned[pl.ds(start, piece, stride=PARTS), :] = block[
                :, index * piece : (index + 1) * piece
            ].T

    place_refs(refs_ref[...].astype(jnp.float32), me)
    for offset in range(1, half):
        source = 2 * behind(offset) + core
        far[offset - 1].wait_recv()
        copy = remote(
            got.at[source], got.at[source], near_send.at[offset], near_recv.at[offset], partner
        )
        copy.start()
        near.append(copy)
        place_refs(unpack(got[source].astype(jnp.float32), share), source)
    for offset in range(half):
        source = 2 * behind(offset) + 1 - core
        near[offset].wait_recv()
        place_refs(unpack(got[source].astype(jnp.float32), share), source)
    for copy in far + near:
        copy.wait_send()

    power = jnp.zeros((rows, SPAN), jnp.float32)
    for q in range(ROT):
        block = turned[q * SPAN : (q + 1) * SPAN, :].T
        power = power + block * block
        block = block.astype(jnp.bfloat16)
        twice[:, q * SPAN : (q + 1) * SPAN] = block
        twice[:, WIDTH + q * SPAN : WIDTH + (q + 1) * SPAN] = block
    quad = 0.5 * lax.dot_general(
        power,
        sw_ref[...],
        (((1,), (0,)), ((), ())),
        precision=lax.Precision.HIGHEST,
        preferred_element_type=jnp.float32,
    )
    col = lax.broadcasted_iota(jnp.int32, (rows, cols), 1)
    used = (lax.rem(col, group) < SIDE * count_img) & (col < SIDE * group)
    quad = jnp.where(used, quad, BIG)

    depth = 4 * SPAN
    for turn in range(ROT):
        scores[turn * rows : (turn + 1) * rows, :] = -quad

    def cross_step(step, carry):
        base = pl.multiple_of(step * depth, depth)
        left = jnp.concatenate(
            [
                twice[:, pl.ds(pl.multiple_of(base + (ROT - turn) * SPAN, SPAN), depth)]
                for turn in range(ROT)
            ],
            axis=0,
        )
        scores[...] += lax.dot_general(
            left,
            feats[:, pl.ds(base, depth)],
            (((1,), (1,)), ((), ())),
            preferred_element_type=jnp.float32,
        )
        return carry

    lax.fori_loop(0, WIDTH // depth, cross_step, 0)

    def max_step(turn, best):
        start = pl.multiple_of(turn * rows, rows)
        return jnp.maximum(best, scores[pl.ds(start, rows), :])

    best = lax.fori_loop(0, ROT, max_step, jnp.full((rows, cols), -BIG, jnp.float32))
    top = fold_lanes(jnp.max(best, axis=0, keepdims=True), count_img, jnp.maximum)

    def exp_step(turn, total):
        start = pl.multiple_of(turn * rows, rows)
        value = jnp.exp(scores[pl.ds(start, rows), :] - top)
        scores[pl.ds(start, rows), :] = value
        return total + value

    total = lax.fori_loop(0, ROT, exp_step, jnp.zeros((rows, cols), jnp.float32))
    norm = fold_lanes(jnp.sum(total, axis=0, keepdims=True), count_img, jnp.add)
    scale = 1.0 / norm

    def post_step(turn, carry):
        start = pl.multiple_of(turn * rows, rows)
        post[pl.ds(start, rows), :] = (scores[pl.ds(start, rows), :] * scale).astype(jnp.bfloat16)
        return carry

    lax.fori_loop(0, ROT, post_step, 0)
    turned_field[...] = lax.dot_general(
        total * scale,
        sw_ref[...],
        (((1,), (1,)), ((), ())),
        precision=lax.Precision.HIGHEST,
        preferred_element_type=jnp.float32,
    ).T

    acc[...] = jnp.zeros_like(acc)
    wide = 2 * SPAN

    def back_step(step, carry):
        base = pl.multiple_of(step * wide, wide)
        oriented = jnp.dot(
            post[...], feats[:, pl.ds(base, wide)], preferred_element_type=jnp.float32
        )
        for turn in range(ROT):
            where = pl.ds(pl.multiple_of(base + (ROT - turn) * SPAN, SPAN), wide)
            acc[:, where] += oriented[turn * rows : (turn + 1) * rows]
        return carry

    lax.fori_loop(0, WIDTH // wide, back_step, 0)
    for q in range(ROT):
        low = acc[:, q * SPAN : (q + 1) * SPAN]
        turned[q * SPAN : (q + 1) * SPAN, :] = (
            low + acc[:, WIDTH + q * SPAN : WIDTH + (q + 1) * SPAN]
        ).T

    def block_for(device):
        parts, weights = [], []
        for index in range(pieces):
            first = device * share + index * piece
            part = lax.div(first, ANG)
            start = lax.rem(first, ANG) * PARTS + part
            parts.append(turned[pl.ds(start, piece, stride=PARTS), :])
            value = turned_field[pl.ds(lax.rem(part, SHELLS), 1), :]
            high = value.astype(jnp.bfloat16).astype(jnp.float32)
            weights += [high, value - high]
        extra = packed - share - len(weights)
        weights.append(jnp.zeros((extra, rows), jnp.float32))
        return jnp.concatenate(parts + weights, axis=0).T

    pairs = []
    for offset in [*range(1, half), 0]:
        slot = ahead(offset)
        pay[offset] = pack(block_for(2 * slot + 1 - core)).astype(jnp.bfloat16)
        copy = remote(
            pay.at[offset], mid.at[offset], pair_send.at[offset], pair_recv.at[offset], partner
        )
        copy.start()
        pairs.append(copy)

    lasts = []
    for index, offset in enumerate([*range(1, half), 0]):
        own = pack(block_for(2 * ahead(offset) + core))
        pairs[index].wait_recv()
        value = own + mid[offset].astype(jnp.float32)
        if offset:
            mixed[offset] = value.astype(jnp.bfloat16)
            copy = remote(
                mixed.at[offset],
                final.at[offset],
                last_send.at[offset],
                last_recv.at[offset],
                2 * ahead(offset) + core,
            )
            copy.start()
            lasts.append(copy)
        else:
            result = value
    for index, copy in enumerate(lasts):
        copy.wait_recv()
        result = result + final[index + 1].astype(jnp.float32)
    result = unpack(result, packed)
    for index in range(pieces):
        place_w = share + 2 * index
        weights = result[:, place_w : place_w + 1] + result[:, place_w + 1 : place_w + 2]
        out_ref[:, index * piece : (index + 1) * piece] = result[
            :, index * piece : (index + 1) * piece
        ] / (weights + 1.0)
    for copy in pairs + lasts:
        copy.wait_send()


def on_device(images, class_refs, sigma2, ctf_group, defocus_bin):
    count_dev = lax.axis_size("img")
    half = count_dev // 2
    count_img = images.shape[0]
    share = class_refs.shape[1]
    cols = -(-SIDE * SLOTS * count_img // LANES) * LANES
    packed = share + 8
    return pl.pallas_call(
        lambda *refs: em_kernel(count_dev, *refs),
        out_shape=jax.ShapeDtypeStruct(class_refs.shape, jnp.float32),
        in_specs=[pl.BlockSpec(memory_space=pltpu.VMEM)] * 7,
        out_specs=pl.BlockSpec(memory_space=pltpu.VMEM),
        scratch_shapes=[
            pltpu.VMEM((cols, WIDTH), jnp.bfloat16),
            pltpu.VMEM((CLASSES, 2 * WIDTH), jnp.bfloat16),
            pltpu.VMEM((ROT * CLASSES, cols), jnp.float32),
            pltpu.VMEM((ROT * CLASSES, cols), jnp.bfloat16),
            pltpu.VMEM((CLASSES, 2 * WIDTH), jnp.float32),
            pltpu.VMEM((WIDTH, count_img), jnp.float32),
            pltpu.VMEM((WIDTH, CLASSES), jnp.float32),
            pltpu.VMEM((SPAN, CLASSES), jnp.float32),
            pltpu.VMEM((SPAN, cols), jnp.float32),
            pltpu.VMEM((4, count_img, WIDTH), jnp.float32),
            pltpu.VMEM((packed_rows(share), LANES), jnp.bfloat16),
            pltpu.VMEM((count_dev, packed_rows(share), LANES), jnp.bfloat16),
            pltpu.VMEM((half, packed_rows(packed), LANES), jnp.bfloat16),
            pltpu.VMEM((half, packed_rows(packed), LANES), jnp.bfloat16),
            pltpu.VMEM((half, packed_rows(packed), LANES), jnp.bfloat16),
            pltpu.VMEM((half, packed_rows(packed), LANES), jnp.bfloat16),
        ]
        + [pltpu.SemaphoreType.DMA((half,))] * 8,
        compiler_params=pltpu.CompilerParams(
            vmem_limit_bytes=60 * 2**20, collective_id=0, has_side_effects=True
        ),
        name="em_step",
    )(
        images,
        class_refs,
        sigma2,
        ctf_group.reshape(1, count_img),
        defocus_bin.reshape(1, count_img),
        jnp.asarray(ctf_lanes()),
        jnp.asarray(phase_parts()),
    )


def solution(mesh):
    in_specs = (
        P(("groups", "img"), None),
        P("groups", "img"),
        P("groups", None),
        P(("groups", "img")),
        P(("groups", "img")),
    )
    out_specs = P("groups", "img")
    return jax.shard_map(
        on_device, mesh=mesh, in_specs=in_specs, out_specs=out_specs, check_vma=False
    )
```

profile of v0, /device:TPU:0, one launch (start us, length us, event | category | flops | bytes accessed | tf_op | source)
XLA Modules:
  0.0 53.5 jit_solution(8160497492496982579)
XLA Ops:
  0.0 52.0 %em_step.1 = f32[48,288]{1,0:T(8,128)} custom-call(bf16[8,4608]{1,0:T(8,128)(2,1)} %refs_0_.1, bf16[48,288]{1,0:T(8,128)(2,1)} %refs_1_.1, f32[16,16]{1,0:T(8,128)} %refs_2_.1, s32[1,8]{1,0:T(1,128)} %bitcast.2, s32[1,8]{1,0:T(1,128)} %bitcast.3, f32[32,128]{1,0:T(8,128)} %constant.4.clone.refs_5_, f32[4,7,4608]{2,1,0:T(8,128)} %constant.5.clone.refs_6_), custom_call_target="tpu_custom_call" | custom-call | tf_op jit(solution)/shard_map/em_step/pallas_call | solution.py:442
  52.0 1.5 %copy.9 = f32[48,288]{1,0:T(8,128)} copy(f32[48,288]{1,0:T(8,128)} %em_step.1) | data formatting | bytes 110592
where the time goes:
time: 53.7 us; the launch traced here: 53.5 us
  Pallas kernels  52 us (97%)
  local copies, waits for them, and re-layouts  1.52 us (3%)
    pallas_call x1, Pallas kernels, on_device(): pl.pallas_call(lambda *refs: em_kernel(count_dev, *refs), out_shape=jax.S...  52 us
    unnamed x1, local copies, waits for them, and re-layouts  1.52 us

commit v1 on v0

v1 whole, which is shorter than its diff:
```python
import math

import jax
import jax.numpy as jnp
import numpy as np
from jax import lax
from jax.experimental import pallas as pl
from jax.experimental.pallas import tpu as pltpu
from jax.sharding import PartitionSpec as P

CLASSES = 48
ROT = 36
SHELLS = 16
ANG = 144
REACH = 3
SHIFTS = 49
BINS = 32
NGROUP = 16

LANES = 128
PARTS = 2 * SHELLS
STEP = ANG // ROT
SPAN = STEP * PARTS
WIDTH = ROT * SPAN
SIDE = 2 * REACH + 1
PAIRS = ROT // 2
TILES = (SHIFTS + 1) // 2
SLOTS = SIDE + 2
BIG = 1e30
EXACT = lax.Precision.HIGHEST


def phase_parts():
    angles = 2.0 * np.pi * np.arange(ANG) / ANG
    radius = (np.arange(SHELLS) + 1.0) / (2.0 * SHELLS)
    tables = []
    for direction in (np.sin(angles), np.cos(angles)):
        for offset in range(1, REACH + 1):
            phase = 2.0 * np.pi * offset * direction[None, :] * radius[:, None]
            both = []
            for cosine, sine in ((np.cos(phase), -np.sin(phase)), (np.cos(phase), np.sin(phase))):
                both.append(np.stack([cosine, sine]))
            table = np.stack(both, axis=1)
            table = table.reshape(2, PARTS, ROT, STEP).transpose(0, 2, 1, 3)
            tables.append(table.reshape(2, ROT, SPAN))
    tables.append(np.ones((2, ROT, SPAN)))
    return np.stack(tables).astype(np.float32)


def ctf_lanes():
    radius = (np.arange(SHELLS) + 1.0) / (2.0 * SHELLS)
    defocus = 1.0 + np.arange(BINS) / BINS
    table = -np.sin(80.0 * defocus[:, None] * radius**2 + 0.1)
    return np.tile(np.repeat(table, STEP, axis=1), (1, 2)).astype(np.float32)


def channel_order():
    table = np.zeros((SPAN, SPAN), np.float32)
    for t in range(STEP):
        for p in range(PARTS):
            table[t * PARTS + p, p * STEP + t] = 1.0
    return table


COS9 = [math.cos(2.0 * math.pi * k / 9.0) for k in range(5)]
SIN9 = [math.sin(2.0 * math.pi * k / 9.0) for k in range(5)]


def even9(first, s1, s2, s3, s4):
    c1, c2 = COS9[1], COS9[2]
    a, b = s1 - s4, s2 - s4
    g1 = c1 * a + c2 * b
    g2 = c2 * (a - b) - c1 * b
    t = s1 + s2 + s4
    w = first + s3
    u = first - 0.5 * s3
    return [w + t, u + g1, u + g2, w - 0.5 * t, u - (g1 + g2)]


def odd9(d1, d2, d3, d4):
    n1, n3, n4 = SIN9[1], SIN9[3], SIN9[4]
    a, b, c = d1 + d2, d2 + d4, d1 - d4
    h1 = n1 * a + n4 * b
    h2 = n1 * c + n4 * a
    e = n3 * d3
    return [h1 + e, h2 - e, n3 * (d1 - d2 + d4), h2 - h1 + e]


def where_q(a, b):
    return (9 * a + 4 * b) % ROT


def dft36(load):
    parts = []
    for a in range(4):
        x = [load(where_q(a, b)) for b in range(9)]
        s = [x[j] + x[9 - j] for j in range(1, 5)]
        d = [x[9 - j] - x[j] for j in range(1, 5)]
        parts.append((even9(x[0], *s), [None] + odd9(*d)))
    y = [part[0][0] for part in parts]
    p, m = y[0] + y[2], y[1] + y[3]
    pairs = [(p + m, p - m), (y[0] - y[2], y[3] - y[1])]
    for g in range(1, 5):
        re = [part[0][g] for part in parts]
        im = [part[1][g] for part in parts]
        rp, rm, ip, im_ = re[0] + re[2], re[0] - re[2], im[0] + im[2], im[0] - im[2]
        sp, sm, jp, jm = re[1] + re[3], re[1] - re[3], im[1] + im[3], im[1] - im[3]
        pairs.append((rp + sp, ip + jp))
        pairs.append((rm + jm, im_ - sm))
        pairs.append((rp - sp, ip - jp))
        pairs.append((rm - jm, im_ + sm))
    return pairs


def idft36(pairs):
    p, m = pairs[0][0] + pairs[0][1], pairs[0][0] - pairs[0][1]
    re, im = pairs[1]
    parts = [[(p + re, None)], [(m - im, None)], [(p - re, None)], [(m + im, None)]]
    for g in range(4):
        (r0, i0), (r1, i1), (r2, i2), (r3, i3) = pairs[2 + 4 * g : 6 + 4 * g]
        rp, rm, ip, im_ = r0 + r2, r0 - r2, i0 + i2, i0 - i2
        sp, sm, jp, jm = r1 + r3, r1 - r3, i1 + i3, i1 - i3
        parts[0].append((rp + sp, ip + jp))
        parts[1].append((rm - jm, im_ + sm))
        parts[2].append((rp - sp, ip - jp))
        parts[3].append((rm + jm, im_ - sm))
    out = [None] * ROT
    for a in range(4):
        y = parts[a]
        even = even9(y[0][0], y[1][0], y[2][0], y[3][0], y[4][0])
        odd = [None] + odd9(y[1][1], y[2][1], y[3][1], y[4][1])
        out[where_q(a, 0)] = even[0]
        for b in range(1, 5):
            out[where_q(a, b)] = even[b] - odd[b]
            out[where_q(a, 9 - b)] = even[b] + odd[b]
    return out


def split(value):
    high = value.astype(jnp.bfloat16)
    return high, (value - high.astype(jnp.float32)).astype(jnp.bfloat16)


def geometry(share):
    piece = min(share, ANG)
    halves = ANG // piece
    pieces = share // piece
    turns = piece // STEP
    width = turns * CLASSES
    padded = -(-(width + CLASSES) // LANES) * LANES
    return piece, halves, pieces, turns, width, padded


def em_kernel(
    count_dev,
    img_ref,
    refs_ref,
    sigma_ref,
    group_ref,
    bin_ref,
    ctf_ref,
    phase_ref,
    perm_ref,
    out_ref,
    turned_img,
    moved,
    fhi,
    flo,
    rhat,
    xs,
    numh,
    flat,
    cols_t,
    fin,
    mine,
    got,
    pay,
    mid,
    mixed,
    final,
    near_send,
    near_recv,
    far_send,
    far_recv,
    pair_send,
    pair_recv,
    last_send,
    last_recv,
):
    rows = CLASSES
    count_img = img_ref.shape[0]
    share = refs_ref.shape[1]
    piece, halves, pieces, turns, width, padded = geometry(share)
    group_rows = STEP * pieces
    count_n = fhi.shape[1]
    half = count_dev // 2
    me = lax.axis_index("img")
    core = lax.rem(me, 2)
    place = lax.div(me, 2)
    partner = me + 1 - 2 * core
    f32, bf16 = jnp.float32, jnp.bfloat16

    def ahead(offset):
        return lax.rem(place + offset, half)

    def behind(offset):
        return lax.rem(place + half - offset, half)

    barrier = pltpu.get_barrier_semaphore()
    for offset in range(1, half):
        pl.semaphore_signal(
            barrier,
            inc=1,
            device_id={"img": 2 * ahead(offset) + core},
            device_id_type=pl.DeviceIdType.MESH,
        )
    pl.semaphore_signal(
        barrier, inc=1, device_id={"img": partner}, device_id_type=pl.DeviceIdType.MESH
    )

    def remote(source, target, send, recv, device):
        return pltpu.make_async_remote_copy(
            src_ref=source,
            dst_ref=target,
            send_sem=send,
            recv_sem=recv,
            device_id={"img": device},
            device_id_type=pl.DeviceIdType.MESH,
        )

    fin[...] = refs_ref[...].astype(f32).T
    turned = []
    for q in range(turns):
        turned.append(
            jnp.concatenate(
                [fin[i * piece + q * STEP : i * piece + (q + 1) * STEP, :] for i in range(pieces)],
                axis=0,
            )
        )
    turned.append(jnp.zeros((group_rows, padded - width), f32))
    own = jnp.concatenate(turned, axis=1).astype(bf16)
    mine[...] = own
    got[me] = own
    pl.semaphore_wait(barrier, half)

    far = [
        remote(
            mine,
            got.at[me],
            far_send.at[offset],
            far_recv.at[offset],
            2 * ahead(offset) + core,
        )
        for offset in range(1, half)
    ]
    near = [remote(mine, got.at[me], near_send.at[0], near_recv.at[0], partner)]
    for copy in far + near:
        copy.start()

    for part in range(PARTS):
        block = img_ref[:, part * ANG : (part + 1) * ANG].astype(f32)
        turned_img[pl.ds(part, ANG, stride=PARTS), :] = block.T

    def pick(ids, table):
        hot = ids == lax.broadcasted_iota(jnp.int32, (table.shape[0], count_img), 0)
        return lax.dot_general(
            hot.astype(f32),
            table,
            (((0,), (0,)), ((), ())),
            precision=EXACT,
            preferred_element_type=f32,
        )

    lane_shell = lax.rem(
        lax.div(lax.broadcasted_iota(jnp.int32, (SHELLS, SPAN), 1), STEP), SHELLS
    )
    spread = (lane_shell == lax.broadcasted_iota(jnp.int32, (SHELLS, SPAN), 0)).astype(f32)
    noise = jnp.dot(
        pick(group_ref[...], sigma_ref[...]), spread, precision=EXACT, preferred_element_type=f32
    )
    ctf = pick(bin_ref[...], ctf_ref[...])
    weight = ctf / noise
    shell_w = jnp.concatenate([ctf * ctf / noise] * (LANES // count_img), axis=0)

    base = jnp.concatenate(
        [turned_img[q * SPAN : (q + 1) * SPAN, :].T for q in range(ROT)], axis=0
    ).astype(bf16)
    base = jnp.dot(base, perm_ref[...], preferred_element_type=f32)
    for q in range(ROT):
        at = slice(q * count_img, (q + 1) * count_img)
        value = base[at] * weight
        other = pltpu.roll(value, SPAN // 2, 1)
        for slot in (REACH, SIDE):
            moved[slot, 0, at, :] = value
            moved[slot, 1, at, :] = other
        moved[SIDE + 1, 0, at, :] = 0.5 * value
        moved[SIDE + 1, 1, at, :] = 0.5 * value
        for offset in range(1, REACH + 1):
            c = phase_ref[REACH + offset - 1, 0, q : q + 1, :]
            s = phase_ref[REACH + offset - 1, 1, q : q + 1, :]
            vc, os, oc, vs = value * c, other * s, other * c, value * s
            moved[REACH + offset, 0, at, :] = vc + os
            moved[REACH + offset, 1, at, :] = oc - vs
            moved[REACH - offset, 0, at, :] = vc - os
            moved[REACH - offset, 1, at, :] = oc + vs

    both = 2 * count_img

    def feature_tile(tile, carry):
        slot = lax.div(tile, REACH)
        entry = lax.rem(tile, REACH) + REACH * (lax.div(tile, REACH * SIDE)) + REACH * lax.div(
            tile, TILES - 1
        )
        start = pl.multiple_of(tile * both, both)

        def load(q):
            at = slice(q * count_img, (q + 1) * count_img)
            a = moved[slot, 0, at, :] * phase_ref[entry, 0, q : q + 1, :]
            b = moved[slot, 1, at, :] * phase_ref[entry, 1, q : q + 1, :]
            return jnp.concatenate([a + b, a - b], axis=0).astype(bf16).astype(f32)

        for j, pair in enumerate(dft36(load)):
            for part, value in enumerate(pair):
                high, low = split(value)
                at = slice(part * SPAN, (part + 1) * SPAN)
                fhi[j, pl.ds(start, both), at] = high
                flo[j, pl.ds(start, both), at] = low
        return carry

    early = TILES * 3 // 5
    lax.fori_loop(0, early, feature_tile, 0)
    for offset in range(1, half):
        source = 2 * behind(offset) + core
        far[offset - 1].wait_recv()
        copy = remote(
            got.at[source], got.at[source], near_send.at[offset], near_recv.at[offset], partner
        )
        copy.start()
        near.append(copy)
    lax.fori_loop(early, TILES, feature_tile, 0)
    for j in range(PAIRS):
        xs[j, :, SPAN * 3 :] = jnp.zeros((2 * rows, xs.shape[2] - SPAN * 3), f32)
    for offset in range(half):
        near[offset].wait_recv()

    for h in range(halves):
        for b in range(padded // LANES):
            block = jnp.concatenate(
                [
                    got[g * halves + h][:, b * LANES : (b + 1) * LANES].astype(f32)
                    for g in range(SPAN // group_rows)
                ],
                axis=0,
            )
            flat[h, b * LANES : (b + 1) * LANES, :] = block.T

    def row_of(q):
        return q // turns, (q % turns) * rows

    power = jnp.zeros((rows, SPAN), f32)
    for q in range(ROT):
        h, start = row_of(q)
        block = flat[h, start : start + rows, :]
        power = power + block * block
    unit = 16

    def refs_tile(tile, carry):
        first = pl.multiple_of(tile * unit, unit)

        def load(q):
            h, start = row_of(q)
            return flat[h, pl.ds(start + first, unit), :]

        low_at = 2 * rows
        for j, (re, im) in enumerate(dft36(load)):
            scale = 1.0 / ROT if j == 0 else 2.0 / ROT
            re, im = scale * re, scale * im
            grid = [[re, im], [-im, re]]
            if j == 0:
                zero = jnp.zeros_like(re)
                grid = [[re, zero], [zero, im]]
            for r in range(2):
                for c in range(2):
                    high, low = split(grid[r][c])
                    at = slice(c * SPAN, (c + 1) * SPAN)
                    rhat[j, pl.ds(first + r * rows, unit), at] = high
                    rhat[j, pl.ds(first + r * rows + low_at, unit), at] = low
        return carry

    lax.fori_loop(0, rows // unit, refs_tile, 0)
    quad = 0.5 * lax.dot_general(
        power, shell_w, (((1,), (1,)), ((), ())), precision=EXACT, preferred_element_type=f32
    )

    def cross_step(j, carry):
        wide = lax.dot_general(
            rhat[j], fhi[j], (((1,), (1,)), ((), ())), preferred_element_type=f32
        )
        rest = lax.dot_general(
            rhat[j, : 2 * rows, :], flo[j], (((1,), (1,)), ((), ())), preferred_element_type=f32
        )
        xs[j, :, :count_n] = wide[: 2 * rows] + wide[2 * rows :] + rest
        return carry

    lax.fori_loop(0, PAIRS, cross_step, 0)

    lane_tiles = xs.shape[2] // LANES
    row_tiles = rows // 8
    used = SHIFTS * count_img
    for k in range(row_tiles):
        for t in range(lane_tiles):
            at = (0, slice(k * 8, (k + 1) * 8), slice(t * LANES, (t + 1) * LANES))
            value = xs[at] - quad[k * 8 : (k + 1) * 8, :]
            if (t + 1) * LANES > used:
                lane = lax.broadcasted_iota(jnp.int32, (8, LANES), 1)
                value = jnp.where(lane < used - t * LANES, value, -BIG)
            xs[at] = value

    def place_of(tile):
        k = pl.multiple_of(lax.div(tile, lane_tiles) * 8, 8)
        t = pl.multiple_of(lax.rem(tile, lane_tiles) * LANES, LANES)
        return k, t

    def load_pairs(k, t):
        return [
            tuple(xs[j, pl.ds(k + part * rows, 8), pl.ds(t, LANES)] for part in range(2))
            for j in range(PAIRS)
        ]

    def score_tile(tile, best):
        k, t = place_of(tile)
        values = idft36(load_pairs(k, t))
        for q, value in enumerate(values):
            xs[q // 2, pl.ds(k + q % 2 * rows, 8), pl.ds(t, LANES)] = value
            best = jnp.maximum(best, value)
        return best

    tiles = row_tiles * lane_tiles
    best = lax.fori_loop(0, tiles, score_tile, jnp.full((8, LANES), -BIG, f32))

    def fold(value, combine):
        reach = count_img
        while reach < LANES:
            value = combine(value, pltpu.roll(value, reach, 1))
            reach *= 2
        return jnp.concatenate([value] * 8, axis=0)

    top = fold(jnp.max(best, axis=0, keepdims=True), jnp.maximum)

    def exp_tile(tile, total):
        k, t = place_of(tile)
        scores = load_pairs(k, t)
        pairs = dft36(lambda q: jnp.exp(scores[q // 2][q % 2] - top))
        for j, pair in enumerate(pairs):
            for part, value in enumerate(pair):
                xs[j, pl.ds(k + part * rows, 8), pl.ds(t, LANES)] = value
        return total + pairs[0][0]

    total = lax.fori_loop(0, tiles, exp_tile, jnp.zeros((8, LANES), f32))
    norm = fold(jnp.sum(total, axis=0, keepdims=True), jnp.add)
    scale = 1.0 / norm
    scale_row = jnp.concatenate([scale[:1]] * lane_tiles, axis=1)

    occupancy = jnp.concatenate(
        [
            sum(
                xs[0, k * 8 : (k + 1) * 8, t * LANES : (t + 1) * LANES] for t in range(lane_tiles)
            )
            * scale
            for k in range(row_tiles)
        ],
        axis=0,
    )
    field = jnp.dot(occupancy, shell_w, precision=EXACT, preferred_element_type=f32)
    high = field.astype(bf16).astype(f32)
    first_lane = lax.rem(lax.broadcasted_iota(jnp.int32, (rows, SPAN), 1), STEP) == 0
    field = jnp.where(first_lane, high, field - high)

    def products(j):
        left = (xs[j] * scale_row).astype(bf16)
        return jnp.dot(left[:, :count_n], fhi[j], preferred_element_type=f32)

    both_real = products(0)
    numh[0, :rows] = 0.5 * both_real[:rows, :SPAN]
    numh[0, rows:] = 0.5 * both_real[rows:, SPAN:]

    def back_step(j, carry):
        value = products(j)
        numh[j, :rows] = value[:rows, :SPAN] + value[rows:, SPAN:]
        numh[j, rows:] = value[:rows, SPAN:] - value[rows:, :SPAN]
        return carry

    lax.fori_loop(1, PAIRS, back_step, 0)

    def number_tile(tile, carry):
        k = pl.multiple_of(tile * 8, 8)
        pairs = [
            tuple(numh[j, pl.ds(k + part * rows, 8), :] for part in range(2)) for j in range(PAIRS)
        ]
        for q, value in enumerate(idft36(pairs)):
            h, start = row_of(q)
            flat[h, pl.ds(start + k, 8), :] = value
        return carry

    lax.fori_loop(0, row_tiles, number_tile, 0)
    for h in range(halves):
        flat[h, width : width + rows, :] = field
        if padded > width + rows:
            flat[h, width + rows :, :] = jnp.zeros((padded - width - rows, SPAN), f32)
        for b in range(padded // LANES):
            block = flat[h, b * LANES : (b + 1) * LANES, :].T
            for g in range(SPAN // group_rows):
                cols_t[h, g, :, b * LANES : (b + 1) * LANES] = block[
                    g * group_rows : (g + 1) * group_rows
                ]

    def block_for(device):
        return cols_t[lax.rem(device, halves), lax.div(device, halves)]

    pairs = []
    for offset in [*range(1, half), 0]:
        slot = ahead(offset)
        pay[offset] = block_for(2 * slot + 1 - core).astype(bf16)
        copy = remote(
            pay.at[offset], mid.at[offset], pair_send.at[offset], pair_recv.at[offset], partner
        )
        copy.start()
        pairs.append(copy)

    lasts = []
    for index, offset in enumerate([*range(1, half), 0]):
        own = block_for(2 * ahead(offset) + core)
        pairs[index].wait_recv()
        value = own + mid[offset].astype(f32)
        if offset:
            mixed[offset] = value.astype(bf16)
            copy = remote(
                mixed.at[offset],
                final.at[offset],
                last_send.at[offset],
                last_recv.at[offset],
                2 * ahead(offset) + core,
            )
            copy.start()
            lasts.append(copy)
        else:
            result = value
    for index, copy in enumerate(lasts):
        copy.wait_recv()
        result = result + final[index + 1].astype(f32)
    weights = result[:, width : width + rows]
    for i in range(pieces):
        inverse = weights[i * STEP : i * STEP + 1] + weights[i * STEP + 1 : i * STEP + 2] + 1.0
        inverse = (2.0 / ROT) / inverse
        for q in range(turns):
            fin[i * piece + q * STEP : i * piece + (q + 1) * STEP, :] = (
                result[i * STEP : (i + 1) * STEP, q * rows : (q + 1) * rows] * inverse
            )
    out_ref[...] = fin[...].T
    for copy in far + near + pairs + lasts:
        copy.wait_send()


def on_device(images, class_refs, sigma2, ctf_group, defocus_bin):
    count_dev = lax.axis_size("img")
    half = count_dev // 2
    count_img = images.shape[0]
    share = class_refs.shape[1]
    piece, halves, pieces, turns, width, padded = geometry(share)
    group_rows = STEP * pieces
    count_n = (SHIFTS + 1) * count_img
    cols = -(-count_n // LANES) * LANES
    travel = pltpu.VMEM((half, group_rows, padded), jnp.bfloat16)
    return pl.pallas_call(
        lambda *refs: em_kernel(count_dev, *refs),
        out_shape=jax.ShapeDtypeStruct(class_refs.shape, jnp.float32),
        in_specs=[pl.BlockSpec(memory_space=pltpu.VMEM)] * 8,
        out_specs=pl.BlockSpec(memory_space=pltpu.VMEM),
        scratch_shapes=[
            pltpu.VMEM((WIDTH, count_img), jnp.float32),
            pltpu.VMEM((SLOTS, 2, ROT * count_img, SPAN), jnp.float32),
            pltpu.VMEM((PAIRS, count_n, 2 * SPAN), jnp.bfloat16),
            pltpu.VMEM((PAIRS, count_n, 2 * SPAN), jnp.bfloat16),
            pltpu.VMEM((PAIRS, 4 * CLASSES, 2 * SPAN), jnp.bfloat16),
            pltpu.VMEM((PAIRS, 2 * CLASSES, cols), jnp.float32),
            pltpu.VMEM((PAIRS, 2 * CLASSES, SPAN), jnp.float32),
            pltpu.VMEM((halves, padded, SPAN), jnp.float32),
            pltpu.VMEM((halves, SPAN // group_rows, group_rows, padded), jnp.float32),
            pltpu.VMEM((share, CLASSES), jnp.float32),
            pltpu.VMEM((group_rows, padded), jnp.bfloat16),
            pltpu.VMEM((count_dev, group_rows, padded), jnp.bfloat16),
            travel,
            travel,
            travel,
            travel,
        ]
        + [pltpu.SemaphoreType.DMA((half,))] * 8,
        compiler_params=pltpu.CompilerParams(
            vmem_limit_bytes=60 * 2**20, collective_id=0, has_side_effects=True
        ),
        name="em_step",
    )(
        images,
        class_refs,
        sigma2,
        ctf_group.reshape(1, count_img),
        defocus_bin.reshape(1, count_img),
        jnp.asarray(ctf_lanes()),
        jnp.asarray(phase_parts()),
        jnp.asarray(channel_order(), dtype=jnp.bfloat16),
    )


def solution(mesh):
    in_specs = (
        P(("groups", "img"), None),
        P("groups", "img"),
        P("groups", None),
        P(("groups", "img")),
        P(("groups", "img")),
    )
    out_specs = P("groups", "img")
    return jax.shard_map(
        on_device, mesh=mesh, in_specs=in_specs, out_specs=out_specs, check_vma=False
    )
```

time: 53.7 us -> 37.3 us (0.69)
  Pallas kernels: 52 us -> 35.6 us
    pallas_call x1, Pallas kernels: 52 us -> 35.6 us  [on_device(): pl.pallas_call(lambda *refs: em_kernel(count_dev, *refs), out_shape=jax.S...]
where the time goes in v1:
time: 37.3 us; the launch traced here: 37.1 us
  Pallas kernels  35.6 us (95%)
  local copies, waits for them, and re-layouts  1.52 us (4%)
    pallas_call x1, Pallas kernels, on_device(): pl.pallas_call(lambda *refs: em_kernel(count_dev, *refs), out_shape=jax.S...  35.6 us
    unnamed x1, local copies, waits for them, and re-layouts  1.52 us

profile of v1, /device:TPU:0, one launch (start us, length us, event | category | flops | bytes accessed | tf_op | source)
XLA Modules:
  0.0 37.1 jit_solution(5284053679044634498)
XLA Ops:
  0.0 35.6 %em_step.1 = f32[48,288]{1,0:T(8,128)} custom-call(bf16[8,4608]{1,0:T(8,128)(2,1)} %refs_0_.1, bf16[48,288]{1,0:T(8,128)(2,1)} %refs_1_.1, f32[16,16]{1,0:T(8,128)} %refs_2_.1, s32[1,8]{1,0:T(1,128)} %bitcast.2, s32[1,8]{1,0:T(1,128)} %bitcast.3, f32[32,128]{1,0:T(8,128)} %constant.6.clone.refs_5_, f32[7,2,36,128]{3,2,1,0:T(8,128)} %constant.7.clone.refs_6_, ...), custom_call_target="tpu_custom_call" | custom-call | tf_op jit(solution)/shard_map/em_step/pallas_call | solution.py:574
  35.6 1.5 %copy.10 = f32[48,288]{1,0:T(8,128)} copy(f32[48,288]{1,0:T(8,128)} %em_step.1) | data formatting | bytes 110592

commit v2 on v1

--- a/solution.py
+++ b/solution.py
@@ -27,6 +27,7 @@
 TILES = (SHIFTS + 1) // 2
 SLOTS = SIDE + 2
 BIG = 1e30
+LOG2E = math.log2(math.e)
 EXACT = lax.Precision.HIGHEST
 
 
@@ -52,14 +53,6 @@
     defocus = 1.0 + np.arange(BINS) / BINS
     table = -np.sin(80.0 * defocus[:, None] * radius**2 + 0.1)
     return np.tile(np.repeat(table, STEP, axis=1), (1, 2)).astype(np.float32)
-
-
-def channel_order():
-    table = np.zeros((SPAN, SPAN), np.float32)
-    for t in range(STEP):
-        for p in range(PARTS):
-            table[t * PARTS + p, p * STEP + t] = 1.0
-    return table
 
 
 COS9 = [math.cos(2.0 * math.pi * k / 9.0) for k in range(5)]
@@ -141,6 +134,51 @@
     return high, (value - high.astype(jnp.float32)).astype(jnp.bfloat16)
 
 
+def image_blocks(img_ref):
+    count = img_ref.shape[0]
+    lane = lax.broadcasted_iota(jnp.int32, (count, LANES), 1)
+    source = [
+        img_ref[:, v * LANES : (v + 1) * LANES].astype(jnp.float32)
+        for v in range(img_ref.shape[1] // LANES)
+    ]
+    per = LANES // STEP
+    rows = []
+    for p in range(PARTS):
+        v, shift = divmod(p * ANG, LANES)
+        value = source[v]
+        if shift:
+            value = jnp.where(
+                lane < LANES - shift,
+                pltpu.roll(source[v], LANES - shift, 1),
+                pltpu.roll(source[v + 1], LANES - shift, 1),
+            )
+        rows.append(value)
+    reach = 1
+    while reach < per:
+        low = (lane & (reach * STEP)) == 0
+        new = list(rows)
+        for p in range(per):
+            if not p & reach:
+                first, second = rows[p], rows[p + reach]
+                new[p] = jnp.where(low, first, pltpu.roll(second, reach * STEP, 1))
+                new[p + reach] = jnp.where(
+                    low, pltpu.roll(first, LANES - reach * STEP, 1), second
+                )
+        rows = new
+        reach *= 2
+    for q in range(per, ROT):
+        value = None
+        for p in range(PARTS):
+            v, start = divmod(p * ANG + q * STEP, LANES)
+            moved = pltpu.roll(source[v], (p * STEP - start) % LANES, 1)
+            if value is None:
+                value = moved
+            else:
+                value = jnp.where(lane < p * STEP, value, moved)
+        rows.append(value)
+    return rows
+
+
 def geometry(share):
     piece = min(share, ANG)
     halves = ANG // piece
@@ -160,9 +198,7 @@
     bin_ref,
     ctf_ref,
     phase_ref,
-    perm_ref,
     out_ref,
-    turned_img,
     moved,
     fhi,
     flo,
@@ -192,7 +228,7 @@
     share = refs_ref.shape[1]
     piece, halves, pieces, turns, width, padded = geometry(share)
     group_rows = STEP * pieces
-    count_n = fhi.shape[1]
+    count_n = fhi.shape[2]
     half = count_dev // 2
     me = lax.axis_index("img")
     core = lax.rem(me, 2)
@@ -257,9 +293,7 @@
     for copy in far + near:
         copy.start()
 
-    for part in range(PARTS):
-        block = img_ref[:, part * ANG : (part + 1) * ANG].astype(f32)
-        turned_img[pl.ds(part, ANG, stride=PARTS), :] = block.T
+    blocks = image_blocks(img_ref)
 
     def pick(ids, table):
         hot = ids == lax.broadcasted_iota(jnp.int32, (table.shape[0], count_img), 0)
@@ -282,13 +316,9 @@
     weight = ctf / noise
     shell_w = jnp.concatenate([ctf * ctf / noise] * (LANES // count_img), axis=0)
 
-    base = jnp.concatenate(
-        [turned_img[q * SPAN : (q + 1) * SPAN, :].T for q in range(ROT)], axis=0
-    ).astype(bf16)
-    base = jnp.dot(base, perm_ref[...], preferred_element_type=f32)
     for q in range(ROT):
         at = slice(q * count_img, (q + 1) * count_img)
-        value = base[at] * weight
+        value = blocks[q] * weight
         other = pltpu.roll(value, SPAN // 2, 1)
         for slot in (REACH, SIDE):
             moved[slot, 0, at, :] = value
@@ -322,9 +352,8 @@
         for j, pair in enumerate(dft36(load)):
             for part, value in enumerate(pair):
                 high, low = split(value)
-                at = slice(part * SPAN, (part + 1) * SPAN)
-                fhi[j, pl.ds(start, both), at] = high
-                flo[j, pl.ds(start, both), at] = low
+                fhi[j, part, pl.ds(start, both), :] = high
+                flo[j, part, pl.ds(start, both), :] = low
         return carry
 
     early = TILES * 3 // 5
@@ -373,7 +402,7 @@
 
         low_at = 2 * rows
         for j, (re, im) in enumerate(dft36(load)):
-            scale = 1.0 / ROT if j == 0 else 2.0 / ROT
+            scale = LOG2E / ROT if j == 0 else 2.0 * LOG2E / ROT
             re, im = scale * re, scale * im
             grid = [[re, im], [-im, re]]
             if j == 0:
@@ -382,27 +411,33 @@
             for r in range(2):
                 for c in range(2):
                     high, low = split(grid[r][c])
-                    at = slice(c * SPAN, (c + 1) * SPAN)
-                    rhat[j, pl.ds(first + r * rows, unit), at] = high
-                    rhat[j, pl.ds(first + r * rows + low_at, unit), at] = low
+                    rhat[j, c, pl.ds(first + r * rows, unit), :] = high
+                    rhat[j, c, pl.ds(first + r * rows + low_at, unit), :] = low
         return carry
 
     lax.fori_loop(0, rows // unit, refs_tile, 0)
-    quad = 0.5 * lax.dot_general(
+    quad = 0.5 * LOG2E * lax.dot_general(
         power, shell_w, (((1,), (1,)), ((), ())), precision=EXACT, preferred_element_type=f32
     )
 
+    def both_halves(ref, j):
+        return jnp.concatenate([ref[j, 0], ref[j, 1]], axis=1)
+
     def cross_step(j, carry):
+        left = both_halves(rhat, j)
         wide = lax.dot_general(
-            rhat[j], fhi[j], (((1,), (1,)), ((), ())), preferred_element_type=f32
+            left, both_halves(fhi, j), (((1,), (1,)), ((), ())), preferred_element_type=f32
         )
         rest = lax.dot_general(
-            rhat[j, : 2 * rows, :], flo[j], (((1,), (1,)), ((), ())), preferred_element_type=f32
+            left[: 2 * rows],
+            both_halves(flo, j),
+            (((1,), (1,)), ((), ())),
+            preferred_element_type=f32,
         )
         xs[j, :, :count_n] = wide[: 2 * rows] + wide[2 * rows :] + rest
         return carry
 
-    lax.fori_loop(0, PAIRS, cross_step, 0)
+    lax.fori_loop(0, PAIRS, cross_step, 0, unroll=True)
 
     lane_tiles = xs.shape[2] // LANES
     row_tiles = rows // 8
@@ -450,7 +485,7 @@
     def exp_tile(tile, total):
         k, t = place_of(tile)
         scores = load_pairs(k, t)
-        pairs = dft36(lambda q: jnp.exp(scores[q // 2][q % 2] - top))
+        pairs = dft36(lambda q: jnp.exp2(scores[q // 2][q % 2] - top))
         for j, pair in enumerate(pairs):
             for part, value in enumerate(pair):
                 xs[j, pl.ds(k + part * rows, 8), pl.ds(t, LANES)] = value
@@ -478,7 +513,7 @@
 
     def products(j):
         left = (xs[j] * scale_row).astype(bf16)
-        return jnp.dot(left[:, :count_n], fhi[j], preferred_element_type=f32)
+        return jnp.dot(left[:, :count_n], both_halves(fhi, j), preferred_element_type=f32)
 
     both_real = products(0)
     numh[0, :rows] = 0.5 * both_real[:rows, :SPAN]
@@ -490,7 +525,7 @@
         numh[j, rows:] = value[:rows, SPAN:] - value[rows:, :SPAN]
         return carry
 
-    lax.fori_loop(1, PAIRS, back_step, 0)
+    lax.fori_loop(1, PAIRS, back_step, 0, unroll=True)
 
     def number_tile(tile, carry):
         k = pl.multiple_of(tile * 8, 8)
@@ -574,14 +609,13 @@
     return pl.pallas_call(
         lambda *refs: em_kernel(count_dev, *refs),
         out_shape=jax.ShapeDtypeStruct(class_refs.shape, jnp.float32),
-        in_specs=[pl.BlockSpec(memory_space=pltpu.VMEM)] * 8,
+        in_specs=[pl.BlockSpec(memory_space=pltpu.VMEM)] * 7,
         out_specs=pl.BlockSpec(memory_space=pltpu.VMEM),
         scratch_shapes=[
-            pltpu.VMEM((WIDTH, count_img), jnp.float32),
             pltpu.VMEM((SLOTS, 2, ROT * count_img, SPAN), jnp.float32),
-            pltpu.VMEM((PAIRS, count_n, 2 * SPAN), jnp.bfloat16),
-            pltpu.VMEM((PAIRS, count_n, 2 * SPAN), jnp.bfloat16),
-            pltpu.VMEM((PAIRS, 4 * CLASSES, 2 * SPAN), jnp.bfloat16),
+            pltpu.VMEM((PAIRS, 2, count_n, SPAN), jnp.bfloat16),
+            pltpu.VMEM((PAIRS, 2, count_n, SPAN), jnp.bfloat16),
+            pltpu.VMEM((PAIRS, 2, 4 * CLASSES, SPAN), jnp.bfloat16),
             pltpu.VMEM((PAIRS, 2 * CLASSES, cols), jnp.float32),
             pltpu.VMEM((PAIRS, 2 * CLASSES, SPAN), jnp.float32),
             pltpu.VMEM((halves, padded, SPAN), jnp.float32),
@@ -607,7 +641,6 @@
         defocus_bin.reshape(1, count_img),
         jnp.asarray(ctf_lanes()),
         jnp.asarray(phase_parts()),
-        jnp.asarray(channel_order(), dtype=jnp.bfloat16),
     )
 
 

time: 37.3 us -> 32.1 us (0.86)
  Pallas kernels: 35.6 us -> 30.4 us
    pallas_call x1, Pallas kernels: 35.6 us -> 30.4 us  [on_device(): pl.pallas_call(lambda *refs: em_kernel(count_dev, *refs), out_shape=jax.S...]
where the time goes in v2:
time: 32.1 us; the launch traced here: 31.9 us
  Pallas kernels  30.4 us (95%)
  local copies, waits for them, and re-layouts  1.52 us (5%)
    pallas_call x1, Pallas kernels, on_device(): pl.pallas_call(lambda *refs: em_kernel(count_dev, *refs), out_shape=jax.S...  30.4 us
    unnamed x1, local copies, waits for them, and re-layouts  1.52 us

profile of v2, /device:TPU:0, one launch (start us, length us, event | category | flops | bytes accessed | tf_op | source)
XLA Modules:
  0.0 31.9 jit_solution(3891354275267660558)
XLA Ops:
  0.0 30.4 %em_step.1 = f32[48,288]{1,0:T(8,128)} custom-call(bf16[8,4608]{1,0:T(8,128)(2,1)} %refs_0_.1, bf16[48,288]{1,0:T(8,128)(2,1)} %refs_1_.1, f32[16,16]{1,0:T(8,128)} %refs_2_.1, s32[1,8]{1,0:T(1,128)} %bitcast.2, s32[1,8]{1,0:T(1,128)} %bitcast.3, f32[32,128]{1,0:T(8,128)} %constant.4.clone.refs_5_, f32[7,2,36,128]{3,2,1,0:T(8,128)} %constant.5.clone.refs_6_), custom_call_target="tpu_custom_call" | custom-call | tf_op jit(solution)/shard_map/em_step/pallas_call | solution.py:609
  30.4 1.5 %copy.9 = f32[48,288]{1,0:T(8,128)} copy(f32[48,288]{1,0:T(8,128)} %em_step.1) | data formatting | bytes 110592

commit v3 on v2

--- a/solution.py
+++ b/solution.py
@@ -179,6 +179,13 @@
     return rows
 
 
+def tree(combine, values):
+    while len(values) > 1:
+        joined = [combine(a, b) for a, b in zip(values[::2], values[1::2])]
+        values = joined + values[len(joined) * 2 :]
+    return values[0]
+
+
 def geometry(share):
     piece = min(share, ANG)
     halves = ANG // piece
@@ -202,8 +209,15 @@
     moved,
     fhi,
     flo,
+    fhi_b,
+    flo_b,
     rhat,
     xs,
+    xs_b,
+    xp,
+    quad_ref,
+    sums,
+    part_sums,
     numh,
     flat,
     cols_t,
@@ -228,7 +242,7 @@
     share = refs_ref.shape[1]
     piece, halves, pieces, turns, width, padded = geometry(share)
     group_rows = STEP * pieces
-    count_n = fhi.shape[2]
+    count_a, count_b = fhi.shape[2], fhi_b.shape[2]
     half = count_dev // 2
     me = lax.axis_index("img")
     core = lax.rem(me, 2)
@@ -336,12 +350,14 @@
 
     both = 2 * count_img
 
-    def feature_tile(tile, carry):
+    tiles_a = count_a // both
+
+    def feature_tile(tile, high_ref, low_ref, first):
         slot = lax.div(tile, REACH)
         entry = lax.rem(tile, REACH) + REACH * (lax.div(tile, REACH * SIDE)) + REACH * lax.div(
             tile, TILES - 1
         )
-        start = pl.multiple_of(tile * both, both)
+        start = pl.multiple_of((tile - first) * both, both)
 
         def load(q):
             at = slice(q * count_img, (q + 1) * count_img)
@@ -352,12 +368,15 @@
         for j, pair in enumerate(dft36(load)):
             for part, value in enumerate(pair):
                 high, low = split(value)
-                fhi[j, part, pl.ds(start, both), :] = high
-                flo[j, part, pl.ds(start, both), :] = low
+                high_ref[j, part, pl.ds(start, both), :] = high
+                low_ref[j, part, pl.ds(start, both), :] = low
+
+    def feature_tile_a(tile, carry):
+        feature_tile(tile, fhi, flo, 0)
         return carry
 
-    early = TILES * 3 // 5
-    lax.fori_loop(0, early, feature_tile, 0)
+    early = tiles_a * 5 // 8
+    lax.fori_loop(0, early, feature_tile_a, 0)
     for offset in range(1, half):
         source = 2 * behind(offset) + core
         far[offset - 1].wait_recv()
@@ -366,9 +385,9 @@
         )
         copy.start()
         near.append(copy)
-    lax.fori_loop(early, TILES, feature_tile, 0)
+    lax.fori_loop(early, tiles_a, feature_tile_a, 0)
     for j in range(PAIRS):
-        xs[j, :, SPAN * 3 :] = jnp.zeros((2 * rows, xs.shape[2] - SPAN * 3), f32)
+        xs_b[j, :, LANES:] = jnp.zeros((2 * rows, LANES), f32)
     for offset in range(half):
         near[offset].wait_recv()
 
@@ -416,62 +435,103 @@
         return carry
 
     lax.fori_loop(0, rows // unit, refs_tile, 0)
-    quad = 0.5 * LOG2E * lax.dot_general(
+    quad_ref[...] = (0.5 * LOG2E) * lax.dot_general(
         power, shell_w, (((1,), (1,)), ((), ())), precision=EXACT, preferred_element_type=f32
     )
 
     def both_halves(ref, j):
         return jnp.concatenate([ref[j, 0], ref[j, 1]], axis=1)
 
-    def cross_step(j, carry):
+    def cross_step(j, high_ref, low_ref, out):
         left = both_halves(rhat, j)
         wide = lax.dot_general(
-            left, both_halves(fhi, j), (((1,), (1,)), ((), ())), preferred_element_type=f32
+            left, both_halves(high_ref, j), (((1,), (1,)), ((), ())), preferred_element_type=f32
         )
         rest = lax.dot_general(
             left[: 2 * rows],
-            both_halves(flo, j),
+            both_halves(low_ref, j),
             (((1,), (1,)), ((), ())),
             preferred_element_type=f32,
         )
-        xs[j, :, :count_n] = wide[: 2 * rows] + wide[2 * rows :] + rest
+        out[j, :, : wide.shape[1]] = wide[: 2 * rows] + wide[2 * rows :] + rest
+
+    steps = PAIRS // (TILES - tiles_a)
+
+    def late_tile(index, carry):
+        for step in range(steps):
+            cross_step(index * steps + step, fhi, flo, xs)
+        feature_tile(tiles_a + index, fhi_b, flo_b, tiles_a)
         return carry
 
-    lax.fori_loop(0, PAIRS, cross_step, 0, unroll=True)
-
-    lane_tiles = xs.shape[2] // LANES
+    lax.fori_loop(0, TILES - tiles_a, late_tile, 0)
+
     row_tiles = rows // 8
-    used = SHIFTS * count_img
-    for k in range(row_tiles):
-        for t in range(lane_tiles):
-            at = (0, slice(k * 8, (k + 1) * 8), slice(t * LANES, (t + 1) * LANES))
-            value = xs[at] - quad[k * 8 : (k + 1) * 8, :]
-            if (t + 1) * LANES > used:
-                lane = lax.broadcasted_iota(jnp.int32, (8, LANES), 1)
-                value = jnp.where(lane < used - t * LANES, value, -BIG)
-            xs[at] = value
-
-    def place_of(tile):
-        k = pl.multiple_of(lax.div(tile, lane_tiles) * 8, 8)
-        t = pl.multiple_of(lax.rem(tile, lane_tiles) * LANES, LANES)
-        return k, t
-
-    def load_pairs(k, t):
-        return [
-            tuple(xs[j, pl.ds(k + part * rows, 8), pl.ds(t, LANES)] for part in range(2))
-            for j in range(PAIRS)
-        ]
-
-    def score_tile(tile, best):
-        k, t = place_of(tile)
-        values = idft36(load_pairs(k, t))
-        for q, value in enumerate(values):
-            xs[q // 2, pl.ds(k + q % 2 * rows, 8), pl.ds(t, LANES)] = value
-            best = jnp.maximum(best, value)
-        return best
-
-    tiles = row_tiles * lane_tiles
-    best = lax.fori_loop(0, tiles, score_tile, jnp.full((8, LANES), -BIG, f32))
+    lane = lax.broadcasted_iota(jnp.int32, (8, LANES), 1)
+    packed_lanes = row_tiles * count_img
+    spots = [(r // 2, r % 2) for r in range(ROT)]
+
+    def load_unit(ref, k, t, j, part):
+        return ref[j, pl.ds(k + part * rows, 8), t * LANES : (t + 1) * LANES]
+
+    def score_unit(pairs, put, carry):
+        top, total = carry
+        values = idft36(pairs)
+        for r, value in enumerate(values):
+            put(*spots[r], value)
+        best = jnp.maximum(top, tree(jnp.maximum, values))
+        total = total * jnp.exp2(top - best)
+        return best, total + tree(jnp.add, [jnp.exp2(value - best) for value in values])
+
+    def score_tile(ref, k, t, carry):
+        pairs = [tuple(load_unit(ref, k, t, j, part) for part in range(2)) for j in range(PAIRS)]
+        pairs[0] = (pairs[0][0] - quad_ref[pl.ds(k, 8), :], pairs[0][1])
+
+        def put(j, part, value):
+            ref[j, pl.ds(k + part * rows, 8), t * LANES : (t + 1) * LANES] = value
+
+        return score_unit(pairs, put, carry)
+
+    steps_b = PAIRS // row_tiles
+
+    def mixed_tile(index, carry):
+        for step in range(steps_b):
+            cross_step(index * steps_b + step, fhi_b, flo_b, xs_b)
+        k = pl.multiple_of(index * 8, 8)
+        return tuple(score_tile(xs, k, t, carry[t]) for t in range(2))
+
+    carry = (jnp.full((8, LANES), -BIG, f32), jnp.zeros((8, LANES), f32))
+    carry = lax.fori_loop(0, row_tiles, mixed_tile, (carry, carry))
+
+    def score_pair(index, carry):
+        k = pl.multiple_of(index * 16, 16)
+        return tuple(score_tile(xs_b, k + 8 * i, 0, carry[i]) for i in range(2))
+
+    carry, other = lax.fori_loop(0, row_tiles // 2, score_pair, carry)
+    best = jnp.maximum(carry[0], other[0])
+    carry = (
+        best,
+        carry[1] * jnp.exp2(carry[0] - best) + other[1] * jnp.exp2(other[0] - best),
+    )
+
+    def side_by_side(load):
+        value = load(0)
+        for k in range(1, row_tiles):
+            value = jnp.where(
+                lane < k * count_img, value, pltpu.roll(load(k), k * count_img, 1)
+            )
+        return value
+
+    pairs = [
+        tuple(side_by_side(lambda k: load_unit(xs_b, k * 8, 1, j, part)) for part in range(2))
+        for j in range(PAIRS)
+    ]
+    shared = side_by_side(lambda k: quad_ref[k * 8 : (k + 1) * 8, :])
+    pairs[0] = (jnp.where(lane < packed_lanes, pairs[0][0] - shared, -BIG), pairs[0][1])
+
+    def put_packed(j, part, value):
+        xp[j, part * 8 : (part + 1) * 8, :] = value
+
+    best, total = score_unit(pairs, put_packed, carry)
 
     def fold(value, combine):
         reach = count_img
@@ -481,51 +541,80 @@
         return jnp.concatenate([value] * 8, axis=0)
 
     top = fold(jnp.max(best, axis=0, keepdims=True), jnp.maximum)
-
-    def exp_tile(tile, total):
-        k, t = place_of(tile)
-        scores = load_pairs(k, t)
-        pairs = dft36(lambda q: jnp.exp2(scores[q // 2][q % 2] - top))
-        for j, pair in enumerate(pairs):
+    norm = fold(jnp.sum(total * jnp.exp2(best - top), axis=0, keepdims=True), jnp.add)
+    scale = 1.0 / norm
+    scale_row = jnp.concatenate([scale[:1], scale[:1]], axis=1)
+    sums[0] = top
+
+    def exp_unit(get, put):
+        high = sums[0]
+        scores = [get(*spot) for spot in spots]
+        for j, pair in enumerate(dft36(lambda q: jnp.exp2(scores[q] - high))):
             for part, value in enumerate(pair):
-                xs[j, pl.ds(k + part * rows, 8), pl.ds(t, LANES)] = value
-        return total + pairs[0][0]
-
-    total = lax.fori_loop(0, tiles, exp_tile, jnp.zeros((8, LANES), f32))
-    norm = fold(jnp.sum(total, axis=0, keepdims=True), jnp.add)
-    scale = 1.0 / norm
-    scale_row = jnp.concatenate([scale[:1]] * lane_tiles, axis=1)
-
-    occupancy = jnp.concatenate(
-        [
-            sum(
-                xs[0, k * 8 : (k + 1) * 8, t * LANES : (t + 1) * LANES] for t in range(lane_tiles)
-            )
-            * scale
-            for k in range(row_tiles)
-        ],
-        axis=0,
-    )
-    field = jnp.dot(occupancy, shell_w, precision=EXACT, preferred_element_type=f32)
+                put(j, part, value)
+
+    def exp_tile(ref, k, t):
+        def put(j, part, value):
+            ref[j, pl.ds(k + part * rows, 8), t * LANES : (t + 1) * LANES] = value
+
+        exp_unit(lambda j, part: load_unit(ref, k, t, j, part), put)
+
+    def exp_pair(index, carry):
+        k = pl.multiple_of(index * 8, 8)
+        for t in range(2):
+            exp_tile(xs, k, t)
+        return carry
+
+    lax.fori_loop(0, row_tiles, exp_pair, 0)
+
+    def products(j, ref, high_ref):
+        count = high_ref.shape[2]
+        left = (ref[j][:, :count] * scale_row[:, :count]).astype(bf16)
+        return jnp.dot(left, both_halves(high_ref, j), preferred_element_type=f32)
+
+    def back_first(index, carry):
+        for step in range(steps_b):
+            j = index * steps_b + step
+            part_sums[j] = products(j, xs, fhi)
+        exp_tile(xs_b, pl.multiple_of(index * 8, 8), 0)
+        return carry
+
+    lax.fori_loop(0, row_tiles, back_first, 0)
+    exp_unit(
+        lambda j, part: xp[j, part * 8 : (part + 1) * 8, :],
+        put_packed,
+    )
+    for j in range(PAIRS):
+        for part in range(2):
+            value = xp[j, part * 8 : (part + 1) * 8, :]
+            for k in range(row_tiles):
+                at = slice(part * rows + k * 8, part * rows + (k + 1) * 8)
+                xs_b[j, at, LANES:] = (
+                    pltpu.roll(value, LANES - k * count_img, 1) if k else value
+                )
+
+    occupancy = []
+    for k in range(row_tiles):
+        at = slice(k * 8, (k + 1) * 8)
+        rest = jnp.where(lane < count_img, xs_b[0, at, LANES:], 0.0)
+        occupancy.append(
+            (xs[0, at, :LANES] + xs[0, at, LANES:] + xs_b[0, at, :LANES] + rest) * scale
+        )
+    field = jnp.dot(
+        jnp.concatenate(occupancy, axis=0), shell_w, precision=EXACT, preferred_element_type=f32
+    )
     high = field.astype(bf16).astype(f32)
     first_lane = lax.rem(lax.broadcasted_iota(jnp.int32, (rows, SPAN), 1), STEP) == 0
     field = jnp.where(first_lane, high, field - high)
 
-    def products(j):
-        left = (xs[j] * scale_row).astype(bf16)
-        return jnp.dot(left[:, :count_n], both_halves(fhi, j), preferred_element_type=f32)
-
-    both_real = products(0)
-    numh[0, :rows] = 0.5 * both_real[:rows, :SPAN]
-    numh[0, rows:] = 0.5 * both_real[rows:, SPAN:]
-
-    def back_step(j, carry):
-        value = products(j)
-        numh[j, :rows] = value[:rows, :SPAN] + value[rows:, SPAN:]
-        numh[j, rows:] = value[:rows, SPAN:] - value[rows:, :SPAN]
-        return carry
-
-    lax.fori_loop(1, PAIRS, back_step, 0, unroll=True)
+    for j in range(PAIRS):
+        value = part_sums[j] + products(j, xs_b, fhi_b)
+        if j:
+            numh[j, :rows] = value[:rows, :SPAN] + value[rows:, SPAN:]
+            numh[j, rows:] = value[:rows, SPAN:] - value[rows:, :SPAN]
+        else:
+            numh[j, :rows] = 0.5 * value[:rows, :SPAN]
+            numh[j, rows:] = 0.5 * value[rows:, SPAN:]
 
     def number_tile(tile, carry):
         k = pl.multiple_of(tile * 8, 8)
@@ -604,7 +693,8 @@
     piece, halves, pieces, turns, width, padded = geometry(share)
     group_rows = STEP * pieces
     count_n = (SHIFTS + 1) * count_img
-    cols = -(-count_n // LANES) * LANES
+    count_a = 2 * LANES
+    count_b = count_n - count_a
     travel = pltpu.VMEM((half, group_rows, padded), jnp.bfloat16)
     return pl.pallas_call(
         lambda *refs: em_kernel(count_dev, *refs),
@@ -613,10 +703,17 @@
         out_specs=pl.BlockSpec(memory_space=pltpu.VMEM),
         scratch_shapes=[
             pltpu.VMEM((SLOTS, 2, ROT * count_img, SPAN), jnp.float32),
-            pltpu.VMEM((PAIRS, 2, count_n, SPAN), jnp.bfloat16),
-            pltpu.VMEM((PAIRS, 2, count_n, SPAN), jnp.bfloat16),
+            pltpu.VMEM((PAIRS, 2, count_a, SPAN), jnp.bfloat16),
+            pltpu.VMEM((PAIRS, 2, count_a, SPAN), jnp.bfloat16),
+            pltpu.VMEM((PAIRS, 2, count_b, SPAN), jnp.bfloat16),
+            pltpu.VMEM((PAIRS, 2, count_b, SPAN), jnp.bfloat16),
             pltpu.VMEM((PAIRS, 2, 4 * CLASSES, SPAN), jnp.bfloat16),
-            pltpu.VMEM((PAIRS, 2 * CLASSES, cols), jnp.float32),
+            pltpu.VMEM((PAIRS, 2 * CLASSES, 2 * LANES), jnp.float32),
+            pltpu.VMEM((PAIRS, 2 * CLASSES, 2 * LANES), jnp.float32),
+            pltpu.VMEM((PAIRS, 16, LANES), jnp.float32),
+            pltpu.VMEM((CLASSES, LANES), jnp.float32),
+            pltpu.VMEM((1, 8, LANES), jnp.float32),
+            pltpu.VMEM((PAIRS, 2 * CLASSES, 2 * SPAN), jnp.float32),
             pltpu.VMEM((PAIRS, 2 * CLASSES, SPAN), jnp.float32),
             pltpu.VMEM((halves, padded, SPAN), jnp.float32),
             pltpu.VMEM((halves, SPAN // group_rows, group_rows, padded), jnp.float32),

time: 32.1 us -> 34.4 us (1.072)
  Pallas kernels: 30.4 us -> 32.7 us
    pallas_call x1, Pallas kernels: 30.4 us -> 32.7 us  [on_device(): pl.pallas_call(lambda *refs: em_kernel(count_dev, *refs), out_shape=jax.S...]
where the time goes in v3:
time: 34.4 us; the launch traced here: 34.3 us
  Pallas kernels  32.7 us (95%)
  local copies, waits for them, and re-layouts  1.52 us (4%)
    pallas_call x1, Pallas kernels, on_device(): pl.pallas_call(lambda *refs: em_kernel(count_dev, *refs), out_shape=jax.S...  32.7 us
    unnamed x1, local copies, waits for them, and re-layouts  1.52 us

profile of v3, /device:TPU:0, one launch (start us, length us, event | category | flops | bytes accessed | tf_op | source)
XLA Modules:
  0.0 34.3 jit_solution(4122110106806143823)
XLA Ops:
  0.0 32.7 %em_step.1 = f32[48,288]{1,0:T(8,128)} custom-call(bf16[8,4608]{1,0:T(8,128)(2,1)} %refs_0_.1, bf16[48,288]{1,0:T(8,128)(2,1)} %refs_1_.1, f32[16,16]{1,0:T(8,128)} %refs_2_.1, s32[1,8]{1,0:T(1,128)} %bitcast.2, s32[1,8]{1,0:T(1,128)} %bitcast.3, f32[32,128]{1,0:T(8,128)} %constant.4.clone.refs_5_, f32[7,2,36,128]{3,2,1,0:T(8,128)} %constant.5.clone.refs_6_), custom_call_target="tpu_custom_call" | custom-call | tf_op jit(solution)/shard_map/em_step/pallas_call | solution.py:699
  32.7 1.5 %copy.9 = f32[48,288]{1,0:T(8,128)} copy(f32[48,288]{1,0:T(8,128)} %em_step.1) | data formatting | bytes 110592

commit v4 on v3

--- a/solution.py
+++ b/solution.py
@@ -198,6 +198,14 @@
 
 def em_kernel(
     count_dev,
+    img_hbm,
+    refs_hbm,
+    sigma_hbm,
+    group_hbm,
+    bin_hbm,
+    ctf_hbm,
+    phase_hbm,
+    out_ref,
     img_ref,
     refs_ref,
     sigma_ref,
@@ -205,19 +213,15 @@
     bin_ref,
     ctf_ref,
     phase_ref,
-    out_ref,
     moved,
     fhi,
     flo,
-    fhi_b,
-    flo_b,
     rhat,
     xs,
     xs_b,
     xp,
     quad_ref,
     sums,
-    part_sums,
     numh,
     flat,
     cols_t,
@@ -236,13 +240,15 @@
     pair_recv,
     last_send,
     last_recv,
+    load_sem,
 ):
     rows = CLASSES
     count_img = img_ref.shape[0]
     share = refs_ref.shape[1]
     piece, halves, pieces, turns, width, padded = geometry(share)
     group_rows = STEP * pieces
-    count_a, count_b = fhi.shape[2], fhi_b.shape[2]
+    count_n = fhi.shape[2]
+    count_a = 2 * LANES
     half = count_dev // 2
     me = lax.axis_index("img")
     core = lax.rem(me, 2)
@@ -278,6 +284,24 @@
             device_id_type=pl.DeviceIdType.MESH,
         )
 
+    loads = [
+        pltpu.make_async_copy(source, target, load_sem.at[index])
+        for index, (source, target) in enumerate(
+            (
+                (refs_hbm, refs_ref),
+                (img_hbm, img_ref),
+                (sigma_hbm, sigma_ref),
+                (group_hbm, group_ref),
+                (bin_hbm, bin_ref),
+                (ctf_hbm, ctf_ref),
+                (phase_hbm, phase_ref),
+            )
+        )
+    ]
+    for copy in loads:
+        copy.start()
+    loads[0].wait()
+
     fin[...] = refs_ref[...].astype(f32).T
     turned = []
     for q in range(turns):
@@ -306,6 +330,9 @@
     near = [remote(mine, got.at[me], near_send.at[0], near_recv.at[0], partner)]
     for copy in far + near:
         copy.start()
+
+    for copy in loads[1:]:
+        copy.wait()
 
     blocks = image_blocks(img_ref)
 
@@ -350,14 +377,12 @@
 
     both = 2 * count_img
 
-    tiles_a = count_a // both
-
-    def feature_tile(tile, high_ref, low_ref, first):
+    def feature_tile(tile, carry):
         slot = lax.div(tile, REACH)
         entry = lax.rem(tile, REACH) + REACH * (lax.div(tile, REACH * SIDE)) + REACH * lax.div(
             tile, TILES - 1
         )
-        start = pl.multiple_of((tile - first) * both, both)
+        start = pl.multiple_of(tile * both, both)
 
         def load(q):
             at = slice(q * count_img, (q + 1) * count_img)
@@ -368,24 +393,36 @@
         for j, pair in enumerate(dft36(load)):
             for part, value in enumerate(pair):
                 high, low = split(value)
-                high_ref[j, part, pl.ds(start, both), :] = high
-                low_ref[j, part, pl.ds(start, both), :] = low
-
-    def feature_tile_a(tile, carry):
-        feature_tile(tile, fhi, flo, 0)
+                fhi[j, part, pl.ds(start, both), :] = high
+                flo[j, part, pl.ds(start, both), :] = low
         return carry
 
-    early = tiles_a * 5 // 8
-    lax.fori_loop(0, early, feature_tile_a, 0)
-    for offset in range(1, half):
+    def relay(offset):
         source = 2 * behind(offset) + core
+        return remote(
+            got.at[source], got.at[source], near_send.at[offset], near_recv.at[offset], partner
+        )
+
+    def relay_step(index, carry):
+        offset = index + 1
+        source = 2 * behind(offset) + core
+        remote(
+            mine, got.at[source], far_send.at[offset], far_recv.at[offset], partner
+        ).wait_recv()
+        relay(offset).start()
+        first = early + index * per_relay
+        lax.fori_loop(first, first + per_relay, feature_tile, 0)
+        return carry
+
+    per_relay = max(1, TILES // (2 * (half - 1)) + 1) if half - 1 <= TILES // 2 else 1
+    relayed = min(half - 1, TILES // per_relay)
+    early = TILES - relayed * per_relay
+    lax.fori_loop(0, early, feature_tile, 0)
+    lax.fori_loop(0, relayed, relay_step, 0)
+    for offset in range(relayed + 1, half):
         far[offset - 1].wait_recv()
-        copy = remote(
-            got.at[source], got.at[source], near_send.at[offset], near_recv.at[offset], partner
-        )
-        copy.start()
-        near.append(copy)
-    lax.fori_loop(early, tiles_a, feature_tile_a, 0)
+        relay(offset).start()
+    near += [relay(offset) for offset in range(1, half)]
     for j in range(PAIRS):
         xs_b[j, :, LANES:] = jnp.zeros((2 * rows, LANES), f32)
     for offset in range(half):
@@ -442,28 +479,20 @@
     def both_halves(ref, j):
         return jnp.concatenate([ref[j, 0], ref[j, 1]], axis=1)
 
-    def cross_step(j, high_ref, low_ref, out):
+    for j in range(PAIRS):
         left = both_halves(rhat, j)
         wide = lax.dot_general(
-            left, both_halves(high_ref, j), (((1,), (1,)), ((), ())), preferred_element_type=f32
+            left, both_halves(fhi, j), (((1,), (1,)), ((), ())), preferred_element_type=f32
         )
         rest = lax.dot_general(
             left[: 2 * rows],
-            both_halves(low_ref, j),
+            both_halves(flo, j),
             (((1,), (1,)), ((), ())),
             preferred_element_type=f32,
         )
-        out[j, :, : wide.shape[1]] = wide[: 2 * rows] + wide[2 * rows :] + rest
-
-    steps = PAIRS // (TILES - tiles_a)
-
-    def late_tile(index, carry):
-        for step in range(steps):
-            cross_step(index * steps + step, fhi, flo, xs)
-        feature_tile(tiles_a + index, fhi_b, flo_b, tiles_a)
-        return carry
-
-    lax.fori_loop(0, TILES - tiles_a, late_tile, 0)
+        value = wide[: 2 * rows] + wide[2 * rows :] + rest
+        xs[j] = value[:, :count_a]
+        xs_b[j, :, : count_n - count_a] = value[:, count_a:]
 
     row_tiles = rows // 8
     lane = lax.broadcasted_iota(jnp.int32, (8, LANES), 1)
@@ -473,14 +502,11 @@
     def load_unit(ref, k, t, j, part):
         return ref[j, pl.ds(k + part * rows, 8), t * LANES : (t + 1) * LANES]
 
-    def score_unit(pairs, put, carry):
-        top, total = carry
+    def score_unit(pairs, put, best):
         values = idft36(pairs)
         for r, value in enumerate(values):
             put(*spots[r], value)
-        best = jnp.maximum(top, tree(jnp.maximum, values))
-        total = total * jnp.exp2(top - best)
-        return best, total + tree(jnp.add, [jnp.exp2(value - best) for value in values])
+        return jnp.maximum(best, tree(jnp.maximum, values))
 
     def score_tile(ref, k, t, carry):
         pairs = [tuple(load_unit(ref, k, t, j, part) for part in range(2)) for j in range(PAIRS)]
@@ -491,27 +517,18 @@
 
         return score_unit(pairs, put, carry)
 
-    steps_b = PAIRS // row_tiles
-
-    def mixed_tile(index, carry):
-        for step in range(steps_b):
-            cross_step(index * steps_b + step, fhi_b, flo_b, xs_b)
+    def score_pair(index, best):
         k = pl.multiple_of(index * 8, 8)
-        return tuple(score_tile(xs, k, t, carry[t]) for t in range(2))
-
-    carry = (jnp.full((8, LANES), -BIG, f32), jnp.zeros((8, LANES), f32))
-    carry = lax.fori_loop(0, row_tiles, mixed_tile, (carry, carry))
-
-    def score_pair(index, carry):
+        return tuple(score_tile(xs, k, t, best[t]) for t in range(2))
+
+    def score_pair_b(index, best):
         k = pl.multiple_of(index * 16, 16)
-        return tuple(score_tile(xs_b, k + 8 * i, 0, carry[i]) for i in range(2))
-
-    carry, other = lax.fori_loop(0, row_tiles // 2, score_pair, carry)
-    best = jnp.maximum(carry[0], other[0])
-    carry = (
-        best,
-        carry[1] * jnp.exp2(carry[0] - best) + other[1] * jnp.exp2(other[0] - best),
-    )
+        return tuple(score_tile(xs_b, k + 8 * i, 0, best[i]) for i in range(2))
+
+    best = jnp.full((8, LANES), -BIG, f32)
+    best = lax.fori_loop(0, row_tiles, score_pair, (best, best))
+    best = lax.fori_loop(0, row_tiles // 2, score_pair_b, best)
+    best = jnp.maximum(*best)
 
     def side_by_side(load):
         value = load(0)
@@ -531,7 +548,7 @@
     def put_packed(j, part, value):
         xp[j, part * 8 : (part + 1) * 8, :] = value
 
-    best, total = score_unit(pairs, put_packed, carry)
+    best = score_unit(pairs, put_packed, best)
 
     def fold(value, combine):
         reach = count_img
@@ -541,49 +558,37 @@
         return jnp.concatenate([value] * 8, axis=0)
 
     top = fold(jnp.max(best, axis=0, keepdims=True), jnp.maximum)
-    norm = fold(jnp.sum(total * jnp.exp2(best - top), axis=0, keepdims=True), jnp.add)
-    scale = 1.0 / norm
-    scale_row = jnp.concatenate([scale[:1], scale[:1]], axis=1)
     sums[0] = top
 
     def exp_unit(get, put):
         high = sums[0]
         scores = [get(*spot) for spot in spots]
-        for j, pair in enumerate(dft36(lambda q: jnp.exp2(scores[q] - high))):
+        pairs = dft36(lambda q: jnp.exp2(scores[q] - high))
+        for j, pair in enumerate(pairs):
             for part, value in enumerate(pair):
                 put(j, part, value)
+        return pairs[0][0]
 
     def exp_tile(ref, k, t):
         def put(j, part, value):
             ref[j, pl.ds(k + part * rows, 8), t * LANES : (t + 1) * LANES] = value
 
-        exp_unit(lambda j, part: load_unit(ref, k, t, j, part), put)
-
-    def exp_pair(index, carry):
+        return exp_unit(lambda j, part: load_unit(ref, k, t, j, part), put)
+
+    def exp_pair(index, total):
         k = pl.multiple_of(index * 8, 8)
-        for t in range(2):
-            exp_tile(xs, k, t)
-        return carry
-
-    lax.fori_loop(0, row_tiles, exp_pair, 0)
-
-    def products(j, ref, high_ref):
-        count = high_ref.shape[2]
-        left = (ref[j][:, :count] * scale_row[:, :count]).astype(bf16)
-        return jnp.dot(left, both_halves(high_ref, j), preferred_element_type=f32)
-
-    def back_first(index, carry):
-        for step in range(steps_b):
-            j = index * steps_b + step
-            part_sums[j] = products(j, xs, fhi)
-        exp_tile(xs_b, pl.multiple_of(index * 8, 8), 0)
-        return carry
-
-    lax.fori_loop(0, row_tiles, back_first, 0)
-    exp_unit(
-        lambda j, part: xp[j, part * 8 : (part + 1) * 8, :],
-        put_packed,
-    )
+        return total + exp_tile(xs, k, 0) + exp_tile(xs, k, 1)
+
+    def exp_pair_b(index, total):
+        k = pl.multiple_of(index * 16, 16)
+        return total + exp_tile(xs_b, k, 0) + exp_tile(xs_b, k + 8, 0)
+
+    total = exp_unit(lambda j, part: xp[j, part * 8 : (part + 1) * 8, :], put_packed)
+    total = lax.fori_loop(0, row_tiles, exp_pair, total)
+    total = lax.fori_loop(0, row_tiles // 2, exp_pair_b, total)
+    norm = fold(jnp.sum(total, axis=0, keepdims=True), jnp.add)
+    scale = 1.0 / norm
+    scale_row = jnp.concatenate([scale[:1]] * 4, axis=1)
     for j in range(PAIRS):
         for part in range(2):
             value = xp[j, part * 8 : (part + 1) * 8, :]
@@ -608,7 +613,9 @@
     field = jnp.where(first_lane, high, field - high)
 
     for j in range(PAIRS):
-        value = part_sums[j] + products(j, xs_b, fhi_b)
+        left = jnp.concatenate([xs[j], xs_b[j]], axis=1)
+        left = (left * scale_row).astype(bf16)[:, :count_n]
+        value = jnp.dot(left, both_halves(fhi, j), preferred_element_type=f32)
         if j:
             numh[j, :rows] = value[:rows, :SPAN] + value[rows:, SPAN:]
             numh[j, rows:] = value[:rows, SPAN:] - value[rows:, :SPAN]
@@ -693,27 +700,32 @@
     piece, halves, pieces, turns, width, padded = geometry(share)
     group_rows = STEP * pieces
     count_n = (SHIFTS + 1) * count_img
-    count_a = 2 * LANES
-    count_b = count_n - count_a
     travel = pltpu.VMEM((half, group_rows, padded), jnp.bfloat16)
+    args = (
+        images,
+        class_refs,
+        sigma2,
+        ctf_group.reshape(1, count_img),
+        defocus_bin.reshape(1, count_img),
+        jnp.asarray(ctf_lanes()),
+        jnp.asarray(phase_parts()),
+    )
     return pl.pallas_call(
         lambda *refs: em_kernel(count_dev, *refs),
         out_shape=jax.ShapeDtypeStruct(class_refs.shape, jnp.float32),
-        in_specs=[pl.BlockSpec(memory_space=pltpu.VMEM)] * 7,
+        in_specs=[pl.BlockSpec(memory_space=pl.ANY)] * 7,
         out_specs=pl.BlockSpec(memory_space=pltpu.VMEM),
-        scratch_shapes=[
+        scratch_shapes=[pltpu.VMEM(arg.shape, arg.dtype) for arg in args]
+        + [
             pltpu.VMEM((SLOTS, 2, ROT * count_img, SPAN), jnp.float32),
-            pltpu.VMEM((PAIRS, 2, count_a, SPAN), jnp.bfloat16),
-            pltpu.VMEM((PAIRS, 2, count_a, SPAN), jnp.bfloat16),
-            pltpu.VMEM((PAIRS, 2, count_b, SPAN), jnp.bfloat16),
-            pltpu.VMEM((PAIRS, 2, count_b, SPAN), jnp.bfloat16),
+            pltpu.VMEM((PAIRS, 2, count_n, SPAN), jnp.bfloat16),
+            pltpu.VMEM((PAIRS, 2, count_n, SPAN), jnp.bfloat16),
             pltpu.VMEM((PAIRS, 2, 4 * CLASSES, SPAN), jnp.bfloat16),
             pltpu.VMEM((PAIRS, 2 * CLASSES, 2 * LANES), jnp.float32),
             pltpu.VMEM((PAIRS, 2 * CLASSES, 2 * LANES), jnp.float32),
             pltpu.VMEM((PAIRS, 16, LANES), jnp.float32),
             pltpu.VMEM((CLASSES, LANES), jnp.float32),
             pltpu.VMEM((1, 8, LANES), jnp.float32),
-            pltpu.VMEM((PAIRS, 2 * CLASSES, 2 * SPAN), jnp.float32),
             pltpu.VMEM((PAIRS, 2 * CLASSES, SPAN), jnp.float32),
             pltpu.VMEM((halves, padded, SPAN), jnp.float32),
             pltpu.VMEM((halves, SPAN // group_rows, group_rows, padded), jnp.float32),
@@ -725,20 +737,13 @@
             travel,
             travel,
         ]
-        + [pltpu.SemaphoreType.DMA((half,))] * 8,
+        + [pltpu.SemaphoreType.DMA((half,))] * 8
+        + [pltpu.SemaphoreType.DMA((len(args),))],
         compiler_params=pltpu.CompilerParams(
             vmem_limit_bytes=60 * 2**20, collective_id=0, has_side_effects=True
         ),
         name="em_step",
-    )(
-        images,
-        class_refs,
-        sigma2,
-        ctf_group.reshape(1, count_img),
-        defocus_bin.reshape(1, count_img),
-        jnp.asarray(ctf_lanes()),
-        jnp.asarray(phase_parts()),
-    )
+    )(*args)
 
 
 def solution(mesh):

time: 34.4 us -> 31.2 us (0.907)
  Pallas kernels: 32.7 us -> 29.5 us
    pallas_call x1, Pallas kernels: 32.7 us -> 29.5 us  [on_device(): pl.pallas_call(lambda *refs: em_kernel(count_dev, *refs), out_shape=jax.S...]
where the time goes in v4:
time: 31.2 us; the launch traced here: 31 us
  Pallas kernels  29.5 us (95%)
  local copies, waits for them, and re-layouts  1.52 us (5%)
    pallas_call x1, Pallas kernels, on_device(): pl.pallas_call(lambda *refs: em_kernel(count_dev, *refs), out_shape=jax.S...  29.5 us
    unnamed x1, local copies, waits for them, and re-layouts  1.52 us

profile of v4, /device:TPU:0, one launch (start us, length us, event | category | flops | bytes accessed | tf_op | source)
XLA Modules:
  0.0 31.0 jit_solution(17981027033460083414)
XLA Ops:
  0.0 29.5 %em_step.1 = f32[48,288]{1,0:T(8,128)} custom-call(bf16[8,4608]{1,0:T(8,128)(2,1)} %refs_0_.1, bf16[48,288]{1,0:T(8,128)(2,1)} %refs_1_.1, f32[16,16]{1,0:T(8,128)} %refs_2_.1, s32[1,8]{1,0:T(1,128)} %bitcast.2, s32[1,8]{1,0:T(1,128)} %bitcast.3, f32[32,128]{1,0:T(8,128)} %constant.4.clone.refs_5_, f32[7,2,36,128]{3,2,1,0:T(8,128)} %constant.5.clone.refs_6_), custom_call_target="tpu_custom_call" | custom-call | tf_op jit(solution)/shard_map/em_step/pallas_call | solution.py:713
  29.5 1.5 %copy.9 = f32[48,288]{1,0:T(8,128)} copy(f32[48,288]{1,0:T(8,128)} %em_step.1) | data formatting | bytes 110592

commit v5 on v4

--- a/solution.py
+++ b/solution.py
@@ -414,7 +414,7 @@
         lax.fori_loop(first, first + per_relay, feature_tile, 0)
         return carry
 
-    per_relay = max(1, TILES // (2 * (half - 1)) + 1) if half - 1 <= TILES // 2 else 1
+    per_relay = 1
     relayed = min(half - 1, TILES // per_relay)
     early = TILES - relayed * per_relay
     lax.fori_loop(0, early, feature_tile, 0)
@@ -508,22 +508,35 @@
             put(*spots[r], value)
         return jnp.maximum(best, tree(jnp.maximum, values))
 
-    def score_tile(ref, k, t, carry):
-        pairs = [tuple(load_unit(ref, k, t, j, part) for part in range(2)) for j in range(PAIRS)]
-        pairs[0] = (pairs[0][0] - quad_ref[pl.ds(k, 8), :], pairs[0][1])
-
+    def put_unit(ref, k, t):
         def put(j, part, value):
             ref[j, pl.ds(k + part * rows, 8), t * LANES : (t + 1) * LANES] = value
 
-        return score_unit(pairs, put, carry)
+        return put
+
+    def score_units(units, best):
+        loaded = []
+        for ref, k, t in units:
+            pairs = [
+                tuple(load_unit(ref, k, t, j, part) for part in range(2)) for j in range(PAIRS)
+            ]
+            pairs[0] = (pairs[0][0] - quad_ref[pl.ds(k, 8), :], pairs[0][1])
+            loaded.append(pairs)
+        solved = [idft36(pairs) for pairs in loaded]
+        for unit, values in zip(units, solved):
+            for r, value in enumerate(values):
+                put_unit(*unit)(*spots[r], value)
+        return tuple(
+            jnp.maximum(old, tree(jnp.maximum, values)) for old, values in zip(best, solved)
+        )
 
     def score_pair(index, best):
         k = pl.multiple_of(index * 8, 8)
-        return tuple(score_tile(xs, k, t, best[t]) for t in range(2))
+        return score_units([(xs, k, 0), (xs, k, 1)], best)
 
     def score_pair_b(index, best):
         k = pl.multiple_of(index * 16, 16)
-        return tuple(score_tile(xs_b, k + 8 * i, 0, best[i]) for i in range(2))
+        return score_units([(xs_b, k, 0), (xs_b, k + 8, 0)], best)
 
     best = jnp.full((8, LANES), -BIG, f32)
     best = lax.fori_loop(0, row_tiles, score_pair, (best, best))

time: 31.2 us -> 30.7 us (0.984)
  Pallas kernels: 29.5 us -> 29 us
    pallas_call x1, Pallas kernels: 29.5 us -> 29 us  [on_device(): pl.pallas_call(lambda *refs: em_kernel(count_dev, *refs), out_shape=jax.S...]
where the time goes in v5:
time: 30.7 us; the launch traced here: 30.5 us
  Pallas kernels  29 us (94%)
  local copies, waits for them, and re-layouts  1.52 us (5%)
    pallas_call x1, Pallas kernels, on_device(): pl.pallas_call(lambda *refs: em_kernel(count_dev, *refs), out_shape=jax.S...  29 us
    unnamed x1, local copies, waits for them, and re-layouts  1.52 us

profile of v5, /device:TPU:0, one launch (start us, length us, event | category | flops | bytes accessed | tf_op | source)
XLA Modules:
  0.0 30.5 jit_solution(14677945340036364859)
XLA Ops:
  0.0 29.0 %em_step.1 = f32[48,288]{1,0:T(8,128)} custom-call(bf16[8,4608]{1,0:T(8,128)(2,1)} %refs_0_.1, bf16[48,288]{1,0:T(8,128)(2,1)} %refs_1_.1, f32[16,16]{1,0:T(8,128)} %refs_2_.1, s32[1,8]{1,0:T(1,128)} %bitcast.2, s32[1,8]{1,0:T(1,128)} %bitcast.3, f32[32,128]{1,0:T(8,128)} %constant.4.clone.refs_5_, f32[7,2,36,128]{3,2,1,0:T(8,128)} %constant.5.clone.refs_6_), custom_call_target="tpu_custom_call" | custom-call | tf_op jit(solution)/shard_map/em_step/pallas_call | solution.py:726
  29.0 1.5 %copy.9 = f32[48,288]{1,0:T(8,128)} copy(f32[48,288]{1,0:T(8,128)} %em_step.1) | data formatting | bytes 110592
